TPU v7x, 32 devices: a whole 2x2x4 slice. The times are simulated.
32 devices in a mesh: grp: 4 (over z), dev: 8 (over y, x, core).
Axes of the slice: x: 2, y: 2, z: 4, core: 2. Of those that a mesh axis runs over, the one named last changes fastest.
Arguments:
- panel: float32 [32768, 512], P(('grp', 'dev')), may hold values from -45 to 45
- signs: int32 [32768], P(('grp', 'dev')), may hold values from 0 to 1
- source_group: int32 [4, 8, 32, 1], P(None, 'dev'), may hold values from 0 to 3; in each aligned block of 32 rows (0 to 31, 32 to 63, ..., all dimensions but the last counted through in order) at most 16 rows name the same one
- source_row: int32 [4, 8, 32], P(None, 'dev'), may hold values from 0 to 1023, as said below
Outputs:
- sketch: float32 [1024, 512], P(('grp', 'dev'))
- conditioned: float32 [32768, 512], P(('grp', 'dev'))
Inputs may be any that keep to these rules, and one draw needn't show every extreme that they name: Among the 32 entries source_group[g, d, :, 0] for one g and d, no group is named more than 16 times, and in some such block one group is named exactly 16 times. source_row[g, d, j] lies in the row band of owner j // 4: source_row[g, d, j] // 128 equals j // 4; the row within the band is free.
All inputs are finite; a program needn't handle non-finite values.
Results may differ from a plain program's by a relative error of at most 0.00013.
Values sent between devices are 32-bit elements; how exact they have to be, the bound alone decides.
A program may use at most 64 MiB of HBM per device.

v0:
```python
import functools
import math
import jax
import jax.numpy as jnp
from jax import lax
from jax.experimental import pallas as pl
from jax.experimental.pallas import tpu as pltpu
from jax.sharding import PartitionSpec as P

BLOCK = 128


def pivot_block(tiles):
    count = len(tiles)
    lane = lax.broadcasted_iota(jnp.int32, (8, BLOCK), 1)
    sub = lax.broadcasted_iota(jnp.int32, (8, BLOCK), 0)
    tiles = list(tiles)
    for p in range(count):
        base = 8 * p
        inside = (lane >= base) & (lane < base + 8)
        cols = {
            q: [jnp.broadcast_to(tiles[q][:, base + t : base + t + 1], (8, BLOCK)) for t in range(8)]
            for q in range(p, count)
        }
        tiles[p] = jnp.where(inside, (lane - base == sub).astype(jnp.float32), tiles[p])
        for q in range(p + 1, count):
            tiles[q] = jnp.where(inside, 0.0, tiles[q])
        diag = jnp.ones((8, BLOCK), jnp.float32)
        for t in range(8):
            pivot = jnp.broadcast_to(cols[p][t][t : t + 1, :], (8, BLOCK))
            diag = jnp.where(sub == t, pivot, diag)
            inverse = 1.0 / pivot
            row = jnp.broadcast_to(tiles[p][t : t + 1, :], (8, BLOCK)) * inverse
            heads = [
                jnp.broadcast_to(cols[p][u][t : t + 1, :], (8, BLOCK)) * inverse for u in range(t + 1, 8)
            ]
            for q in range(p, count):
                coef = cols[q][t]
                if q == p:
                    coef = jnp.where(sub > t, coef, 0.0)
                for place, u in enumerate(range(t + 1, 8)):
                    cols[q][u] = cols[q][u] - coef * heads[place]
                tiles[q] = tiles[q] - coef * row
        tiles[p] = tiles[p] * lax.rsqrt(diag)
    return tiles


def inverse_factor(work):
    size = work.shape[0]
    rowi = lax.broadcasted_iota(jnp.int32, (BLOCK, BLOCK), 0)
    coli = lax.broadcasted_iota(jnp.int32, (BLOCK, BLOCK), 1)
    wide = lax.broadcasted_iota(jnp.int32, (BLOCK, size), 1)

    def step(k, carry):
        start = pl.multiple_of(k * BLOCK, BLOCK)
        here = pl.ds(start, BLOCK)
        tiles = [
            work[pl.ds(pl.multiple_of(start + 8 * p, 8), 8), here] for p in range(BLOCK // 8)
        ]
        tiles = pivot_block(tiles)
        own = jnp.where(rowi >= coli, jnp.concatenate(tiles, axis=0), 0.0)
        rows = split_matmul(halves(own), halves(work[here, :]), ((1,), (0,)))
        work[here, :] = rows
        work[here, here] = own
        rows = work[here, :]

        @pl.when(start + BLOCK < size)
        def _():
            work[:, here] = jnp.where(
                lax.broadcasted_iota(jnp.int32, (size, BLOCK), 0) >= start + BLOCK, 0.0, work[:, here]
            )
            left = jnp.where(wide >= start + BLOCK, rows, 0.0)
            work[...] = work[...] - split_matmul(halves(left), halves(rows), ((0,), (0,)))

        work[here, :] = jnp.where(wide < start + BLOCK, rows, 0.0)
        return carry

    lax.fori_loop(0, size // BLOCK, step, 0)


def add_ridge(gram, sketch_total):
    size = gram.shape[0]
    rowi = lax.broadcasted_iota(jnp.int32, (size, size), 0)
    coli = lax.broadcasted_iota(jnp.int32, (size, size), 1)
    return gram / sketch_total + jnp.where(rowi == coli, 0.001, 0.0)


def halves(value):
    high = value.astype(jnp.bfloat16)
    return high, (value - high.astype(jnp.float32)).astype(jnp.bfloat16)


def split_matmul(a, b, dims):
    dot = functools.partial(
        lax.dot_general, dimension_numbers=(dims, ((), ())), preferred_element_type=jnp.float32
    )
    return dot(a[0], b[0]) + (dot(a[0], b[1]) + dot(a[1], b[0]))


def finish(work, panel_ref, out_ref):
    rows, columns = panel_ref.shape
    part = columns // 2
    for base in (0, part):
        deep = base + part
        factor = halves(work[base : base + part, 0:deep])
        out_ref[:, base : base + part] = split_matmul(
            halves(panel_ref[:, 0:deep]), factor, ((1,), (1,))
        )


def gram_kernel(sketch_total, sketch_ref, panel_ref, own_ref, out_ref, work):
    own_ref[...] = sketch_ref[0 : own_ref.shape[0], :]
    sketch = halves(sketch_ref[...])
    work[...] = add_ridge(split_matmul(sketch, sketch, ((0,), (0,))), sketch_total)
    inverse_factor(work)
    finish(work, panel_ref, out_ref)


def from_gram_kernel(sketch_total, gram_ref, panel_ref, out_ref, work):
    work[...] = add_ridge(gram_ref[...], sketch_total)
    inverse_factor(work)
    finish(work, panel_ref, out_ref)


def flip(index, mask):
    bit = 1
    while bit <= mask:
        if mask & bit:
            index = index + bit - 2 * bit * lax.rem(lax.div(index, bit), 2)
        bit = 2 * bit
    return index


def parity_sign(value, bits):
    span = 1
    while span < bits:
        span = span * 2
    while span > 1:
        span = span // 2
        value = value ^ (value >> span)
    return (1 - 2 * (value & 1)).astype(jnp.float32)


def sketch_kernel(
    groups, per_owner, scale, panel_ref, signs_ref, group_ref, row_ref, whole_ref,
    lists, values, high, low, choice, acc, from_core, from_first, from_second, from_group, send, recv,
):
    devices = 8
    rows_here, columns = panel_ref.shape
    part = columns // 4
    lefts, rights = (pl.ds(0, part), pl.ds(2 * part, part)), (pl.ds(part, part), pl.ds(3 * part, part))
    both = (pl.ds(0, 2 * part), pl.ds(2 * part, 2 * part))
    band = groups * devices * per_owner
    share = devices * per_owner
    me = lax.axis_index("dev")
    here = lax.axis_index("grp")

    barrier = pltpu.get_barrier_semaphore()
    for mask in range(1, devices):
        pl.semaphore_signal(
            barrier, inc=1, device_id={"dev": flip(me, mask)}, device_id_type=pl.DeviceIdType.MESH
        )
    for mask in range(1, groups):
        pl.semaphore_signal(
            barrier, inc=1, device_id={"grp": flip(here, mask)}, device_id_type=pl.DeviceIdType.MESH
        )
    pl.semaphore_wait(barrier, devices + groups - 2)

    taken = []

    def transfer(source, target, axis, mask):
        place = len(taken)
        taken.append(place)
        peer = flip(me if axis == "dev" else here, mask)
        copy = pltpu.make_async_remote_copy(
            src_ref=source,
            dst_ref=target,
            send_sem=send.at[place],
            recv_sem=recv.at[place],
            device_id={axis: peer},
            device_id_type=pl.DeviceIdType.MESH,
        )
        copy.start()
        return copy

    sends = []
    listed = [transfer(group_ref, lists.at[0, mask], "dev", mask) for mask in range(1, devices)]
    listed += [transfer(row_ref, lists.at[1, mask], "dev", mask) for mask in range(1, devices)]
    top = panel_ref[...].astype(jnp.bfloat16)
    high[...] = top
    low[...] = (panel_ref[...] - top.astype(jnp.float32)).astype(jnp.bfloat16)
    lists[0, 0] = group_ref[...]
    lists[1, 0] = row_ref[...]
    for copy in listed:
        copy.wait_recv()
    sends += listed

    for slot in range(devices):
        values[slot * groups : (slot + 1) * groups, :] = (
            lists[0, slot] * devices + flip(me, slot)
        ) * rows_here + lists[1, slot]
    total = devices * band
    width = devices * per_owner
    place = lax.broadcasted_iota(jnp.int32, (total, width), 0)
    entry = lax.broadcasted_iota(jnp.int32, (total, width), 1)
    wanted = ((place // band) ^ me) * per_owner + place % per_owner
    spread = lax.dot_general(
        (entry == wanted).astype(jnp.float32),
        values[...].astype(jnp.float32),
        (((1,), (1,)), ((), ())),
        precision=lax.Precision.HIGHEST,
        preferred_element_type=jnp.float32,
    )
    place = lax.broadcasted_iota(jnp.int32, (total, devices * groups), 0)
    held = lax.broadcasted_iota(jnp.int32, (total, devices * groups), 1)
    source = (((place // per_owner) % devices) ^ me) * groups + (((place // share) % groups) ^ here)
    choice[...] = jnp.sum(jnp.where(held == source, spread, 0.0), axis=1, keepdims=True).astype(jnp.int32)

    def mixed(chunk):
        pick = jnp.broadcast_to(choice[chunk * band : (chunk + 1) * band, :], (band, 128))
        lane = lax.broadcasted_iota(jnp.int32, (band, 128), 1)
        rank = here * devices + me
        above = parity_sign((pick // rows_here) & rank, (groups * devices).bit_length() - 1)
        table = [parity_sign(pick & lane, 7) * above]
        bit = 7
        while 128 * len(table) < rows_here:
            turn = (1 - 2 * ((pick >> bit) & 1)).astype(jnp.float32)
            table = table + [part * turn for part in table]
            bit = bit + 1
        turns = (1 - 2 * signs_ref[...]).astype(jnp.float32)
        table = [part * turns[i : i + 1, :] for i, part in enumerate(table)]
        table = jnp.concatenate([part.astype(jnp.bfloat16) for part in table], axis=1)
        dims = (((1,), (0,)), ((), ()))
        return lax.dot_general(
            table, high[...], dims, preferred_element_type=jnp.float32
        ) + lax.dot_general(table, low[...], dims, preferred_element_type=jnp.float32)

    core = {}
    for chunk in (7, 3, 5, 1):
        acc[chunk] = mixed(chunk)
        core[chunk - 1] = transfer(acc.at[chunk], from_core.at[chunk // 2], "dev", 1)
    first, second = {}, {}

    def send_first(chunk, turn):
        left, right = lefts[turn], rights[turn]
        if chunk & 2:
            first[turn, "left", chunk - 2] = transfer(
                acc.at[chunk, :, left], from_first.at[chunk // 4, :, left], "dev", 2
            )
        if chunk & 4:
            first[turn, "right", chunk - 4] = transfer(
                acc.at[chunk, :, right], from_first.at[(chunk & 2) // 2, :, right], "dev", 4
            )

    for chunk in (6, 2, 4, 0):
        acc[chunk] = mixed(chunk)
        core[chunk].wait_recv()
        acc[chunk] = acc[chunk] + from_core[chunk // 2]
        send_first(chunk, 0)
        if chunk == 4:
            for late in (6, 2, 4):
                send_first(late, 1)
    for turn in range(2):
        left, right = lefts[turn], rights[turn]
        first[turn, "left", 4].wait_recv()
        acc[4, :, left] = acc[4, :, left] + from_first[1, :, left]
        second[turn, "left"] = transfer(acc.at[4, :, left], from_second.at[:, left], "dev", 4)
        first[turn, "right", 2].wait_recv()
        acc[2, :, right] = acc[2, :, right] + from_first[1, :, right]
        second[turn, "right"] = transfer(acc.at[2, :, right], from_second.at[:, right], "dev", 2)
    summed = []
    for turn in range(2):
        first[turn, "left", 0].wait_recv()
        first[turn, "right", 0].wait_recv()
        second[turn, "left"].wait_recv()
        second[turn, "right"].wait_recv()
        columns_now = both[turn]
        acc[0, :, columns_now] = (
            acc[0, :, columns_now] + from_first[0, :, columns_now] + from_second[:, columns_now]
        )
        summed.append([
            transfer(
                acc.at[0, pl.ds(block * share, share), columns_now],
                from_group.at[block, :, columns_now],
                "grp",
                block,
            )
            for block in range(1, groups)
        ])
    sends += list(core.values()) + list(first.values()) + list(second.values())

    spread_out = []
    for turn in range(2):
        columns_now = both[turn]
        result = acc[0, 0:share, columns_now]
        for block in range(1, groups):
            summed[turn][block - 1].wait_recv()
            result = result + from_group[block, :, columns_now]
        whole_ref[0, 0:share, columns_now] = result * scale
        spread_out.append([
            transfer(
                whole_ref.at[0, pl.ds(0, share), columns_now],
                whole_ref.at[0, pl.ds(block * share, share), columns_now],
                "grp",
                block,
            )
            for block in range(1, groups)
        ])
        sends += summed[turn]
    out, relay, last = [], [], []

    def hand_over(chunk, turn):
        columns_now = both[turn]
        last.append(
            transfer(whole_ref.at[chunk, :, columns_now], whole_ref.at[chunk + 1, :, columns_now], "dev", 1)
        )

    for turn in range(2):
        left, right = lefts[turn], rights[turn]
        for copy in spread_out[turn]:
            copy.wait_recv()
        out.append([
            transfer(whole_ref.at[0, :, left], whole_ref.at[4, :, left], "dev", 4),
            transfer(whole_ref.at[0, :, right], whole_ref.at[2, :, right], "dev", 2),
            transfer(whole_ref.at[0, :, left], whole_ref.at[2, :, left], "dev", 2),
            transfer(whole_ref.at[0, :, right], whole_ref.at[4, :, right], "dev", 4),
        ])
        hand_over(0, turn)
        sends += spread_out[turn] + out[turn]
    for turn in range(2):
        left, right = lefts[turn], rights[turn]
        out[turn][0].wait_recv()
        relay.append(transfer(whole_ref.at[4, :, left], whole_ref.at[6, :, left], "dev", 2))
        out[turn][1].wait_recv()
        relay.append(transfer(whole_ref.at[2, :, right], whole_ref.at[6, :, right], "dev", 4))
        out[turn][2].wait_recv()
        hand_over(2, turn)
        out[turn][3].wait_recv()
        hand_over(4, turn)
    for turn in range(2):
        relay[2 * turn].wait_recv()
        relay[2 * turn + 1].wait_recv()
        hand_over(6, turn)
    for copy in last:
        copy.wait_recv()
    sends += relay + last
    for copy in sends:
        copy.wait_send()


def kernel_sketch(panel, signs, source_group, source_row, groups, devices):
    rows_here, columns = panel.shape
    per_owner = source_row.shape[2] // devices
    band = groups * devices * per_owner
    share = devices * per_owner
    scale = 1.0 / math.sqrt(rows_here * devices * groups)
    vmem = pl.BlockSpec(memory_space=pltpu.VMEM)
    f32 = jnp.float32
    whole = pl.pallas_call(
        functools.partial(sketch_kernel, groups, per_owner, scale),
        out_shape=jax.ShapeDtypeStruct((devices, band, columns), f32),
        in_specs=[vmem] * 4,
        out_specs=vmem,
        scratch_shapes=[
            pltpu.VMEM((2, devices, groups, share), jnp.int32),
            pltpu.VMEM((devices * groups, share), jnp.int32),
            pltpu.VMEM((rows_here, columns), jnp.bfloat16),
            pltpu.VMEM((rows_here, columns), jnp.bfloat16),
            pltpu.VMEM((devices * band, 1), jnp.int32),
            pltpu.VMEM((devices, band, columns), f32),
            pltpu.VMEM((devices // 2, band, columns), f32),
            pltpu.VMEM((2, band, columns), f32),
            pltpu.VMEM((band, columns), f32),
            pltpu.VMEM((groups, share, columns), f32),
            pltpu.SemaphoreType.DMA((72,)),
            pltpu.SemaphoreType.DMA((72,)),
        ],
        compiler_params=pltpu.CompilerParams(collective_id=0, has_side_effects=True),
        name="sketch",
    )(
        panel,
        signs.reshape(rows_here // 128, 128),
        source_group.reshape(groups, share),
        source_row.reshape(groups, share),
    )
    return whole.reshape(devices * band, columns)


def bit_parity(value, bits):
    total = jnp.zeros_like(value)
    for bit_place in range(bits):
        total = total + (value >> bit_place & 1)
    return total & 1


def sylvester(order):
    index = jnp.arange(order, dtype=jnp.int32)
    parity = bit_parity(index[:, None] & index[None, :], order.bit_length())
    return (1 - 2 * parity).astype(jnp.float32)


def general_sketch(panel, signs, source_group, source_row):
    rows_here = panel.shape[0]
    columns = panel.shape[1]
    groups = lax.axis_size("grp")
    devices = lax.axis_size("dev")
    group_here = lax.axis_index("grp")
    highest = lax.Precision.HIGHEST
    flipped = panel * (1 - 2 * signs).astype(jnp.float32)[:, None]
    local = jnp.dot(
        sylvester(rows_here), flipped, precision=highest, preferred_element_type=jnp.float32
    )
    dev_table = sylvester(devices)
    mixed = jnp.einsum(
        "ed,dbc->ebc",
        dev_table,
        lax.all_to_all(
            local.reshape(devices, rows_here // devices, columns),
            "dev",
            split_axis=0,
            concat_axis=0,
            tiled=True,
        ),
        precision=highest,
    )
    inner = mixed
    inner = inner.reshape(rows_here, columns)
    chosen_group = source_group[:, 0, :, 0]
    chosen_row = source_row[:, 0, :]
    width = chosen_group.shape[1]
    per_owner = width // devices
    band_size = rows_here // devices
    dev_here = lax.axis_index("dev")
    stacked = jnp.stack([chosen_group, chosen_row]).reshape(2, groups, devices, per_owner)
    lists = lax.all_to_all(stacked, "dev", split_axis=2, concat_axis=2, tiled=True)
    band_group = lists[0].reshape(-1)
    band_row = lists[1].reshape(-1)
    flat_place = jnp.arange(groups * devices * per_owner, dtype=jnp.int32)
    source_dev = flat_place // per_owner % devices
    flat_index = source_dev * band_size + band_row - dev_here * band_size
    parity = bit_parity(band_group & group_here, groups.bit_length())
    factor = (1 - 2 * parity).astype(jnp.float32)
    gathered = lax.psum_scatter(
        inner[flat_index] * factor[:, None], "grp", scatter_dimension=0, tiled=True
    )
    panel_total = rows_here * devices * groups
    sketch = gathered * (1.0 / math.sqrt(panel_total))
    sketch_total = sketch.shape[0] * devices * groups
    partial_gram = jnp.dot(sketch.T, sketch, precision=highest, preferred_element_type=jnp.float32)
    return sketch, lax.psum(partial_gram, ("grp", "dev"))


def on_device(panel, signs, source_group, source_row):
    rows_here, columns = panel.shape
    groups = lax.axis_size("grp")
    devices = lax.axis_size("dev")
    width = source_row.shape[2]
    sketch_total = groups * devices * width
    fits = groups & (groups - 1) == 0 and groups * width == 128 and columns % 512 == 0 and rows_here % 128 == 0
    if devices == 8 and fits and rows_here & (rows_here - 1) == 0:
        pieces = kernel_sketch(panel, signs, source_group, source_row, groups, devices)
        kernel, shapes = gram_kernel, [(width, columns), (rows_here, columns)]
    else:
        sketch, pieces = general_sketch(panel, signs, source_group, source_row)
        kernel, shapes = from_gram_kernel, [(rows_here, columns)]
    *own, conditioned = pl.pallas_call(
        functools.partial(kernel, sketch_total),
        out_shape=[jax.ShapeDtypeStruct(shape, jnp.float32) for shape in shapes],
        in_specs=[pl.BlockSpec(memory_space=pltpu.VMEM)] * 2,
        out_specs=[pl.BlockSpec(memory_space=pltpu.VMEM)] * len(shapes),
        scratch_shapes=[pltpu.VMEM((columns, columns), jnp.float32)],
        name="factor",
    )(pieces, panel)
    if own:
        sketch = own[0]
    return (sketch, conditioned)


def solution(mesh):
    return jax.shard_map(
        on_device,
        mesh=mesh,
        in_specs=(
            P(("grp", "dev"), None),
            P(("grp", "dev")),
            P(None, "dev", None, None),
            P(None, "dev", None),
        ),
        out_specs=(P(("grp", "dev"), None), P(("grp", "dev"), None)),
        check_vma=False,
    )
```

profile of v0, /device:TPU:0, one launch (start us, length us, event | category | flops | bytes accessed | tf_op | source)
XLA Modules:
  0.0 76.1 jit_solution(871234609910610187)
XLA Ops:
  0.6 49.2 %sketch.1 = f32[8,128,512]{2,1,0:T(8,128)} custom-call(f32[1024,512]{1,0:T(8,128)} %panel_ref.3, s32[8,128]{1,0:T(8,128)} %bitcast.5, s32[4,32]{1,0:T(4,128)} %bitcast.6, s32[4,32]{1,0:T(4,128)} %bitcast.7), custom_call_target="tpu_custom_call" | custom-call | tf_op jit(solution)/shard_map/sketch/pallas_call | solution.py:359
  49.8 26.3 %factor.1 = (f32[32,512]{1,0:T(8,128)}, f32[1024,512]{1,0:T(8,128)}) custom-call(f32[1024,512]{1,0:T(8,128)} %bitcast.4, f32[1024,512]{1,0:T(8,128)} %panel_ref.3), custom_call_target="tpu_custom_call" | custom-call | tf_op jit(solution)/shard_map/factor/pallas_call | solution.py:466
where the time goes:
time: 76.3 us; the launch traced here: 76.1 us
  Pallas kernels  75.5 us (99%)
    pallas_call x1, Pallas kernels, kernel_sketch(): pl.pallas_call(functools.partial(sketch_kernel, groups, per_owner, scale)...  49.2 us
    pallas_call x1, Pallas kernels, on_device(): pl.pallas_call(functools.partial(kernel, sketch_total), out_shape=[jax.Sh...  26.3 us

commit v1 on v0

v1 whole, which is shorter than its diff:
```python
import functools
import math
import jax
import jax.numpy as jnp
from jax import lax
from jax.experimental import pallas as pl
from jax.experimental.pallas import tpu as pltpu
from jax.sharding import PartitionSpec as P

BLOCK = 128


def pivot_block(tiles):
    count = len(tiles)
    lane = lax.broadcasted_iota(jnp.int32, (8, BLOCK), 1)
    sub = lax.broadcasted_iota(jnp.int32, (8, BLOCK), 0)
    tiles = list(tiles)
    for p in range(count):
        base = 8 * p
        inside = (lane >= base) & (lane < base + 8)
        cols = {
            q: [jnp.broadcast_to(tiles[q][:, base + t : base + t + 1], (8, BLOCK)) for t in range(8)]
            for q in range(p, count)
        }
        tiles[p] = jnp.where(inside, (lane - base == sub).astype(jnp.float32), tiles[p])
        for q in range(p + 1, count):
            tiles[q] = jnp.where(inside, 0.0, tiles[q])
        diag = jnp.ones((8, BLOCK), jnp.float32)
        for t in range(8):
            pivot = jnp.broadcast_to(cols[p][t][t : t + 1, :], (8, BLOCK))
            diag = jnp.where(sub == t, pivot, diag)
            inverse = 1.0 / pivot
            row = jnp.broadcast_to(tiles[p][t : t + 1, :], (8, BLOCK)) * inverse
            heads = [
                jnp.broadcast_to(cols[p][u][t : t + 1, :], (8, BLOCK)) * inverse for u in range(t + 1, 8)
            ]
            for q in range(p, count):
                coef = cols[q][t]
                if q == p:
                    coef = jnp.where(sub > t, coef, 0.0)
                for place, u in enumerate(range(t + 1, 8)):
                    cols[q][u] = cols[q][u] - coef * heads[place]
                tiles[q] = tiles[q] - coef * row
        tiles[p] = tiles[p] * lax.rsqrt(diag)
    return tiles


def inverse_factor(work):
    size = work.shape[0]
    rowi = lax.broadcasted_iota(jnp.int32, (BLOCK, BLOCK), 0)
    coli = lax.broadcasted_iota(jnp.int32, (BLOCK, BLOCK), 1)
    wide = lax.broadcasted_iota(jnp.int32, (BLOCK, size), 1)

    def step(k, carry):
        start = pl.multiple_of(k * BLOCK, BLOCK)
        here = pl.ds(start, BLOCK)
        tiles = [
            work[pl.ds(pl.multiple_of(start + 8 * p, 8), 8), here] for p in range(BLOCK // 8)
        ]
        tiles = pivot_block(tiles)
        own = jnp.where(rowi >= coli, jnp.concatenate(tiles, axis=0), 0.0)
        rows = split_matmul(halves(own), halves(work[here, :]), ((1,), (0,)))
        work[here, :] = rows
        work[here, here] = own
        rows = work[here, :]

        @pl.when(start + BLOCK < size)
        def _():
            work[:, here] = jnp.where(
                lax.broadcasted_iota(jnp.int32, (size, BLOCK), 0) >= start + BLOCK, 0.0, work[:, here]
            )
            left = jnp.where(wide >= start + BLOCK, rows, 0.0)
            work[...] = work[...] - split_matmul(halves(left), halves(rows), ((0,), (0,)))

        work[here, :] = jnp.where(wide < start + BLOCK, rows, 0.0)
        return carry

    lax.fori_loop(0, size // BLOCK, step, 0)


def add_ridge(gram, sketch_total):
    size = gram.shape[0]
    rowi = lax.broadcasted_iota(jnp.int32, (size, size), 0)
    coli = lax.broadcasted_iota(jnp.int32, (size, size), 1)
    return gram / sketch_total + jnp.where(rowi == coli, 0.001, 0.0)


def halves(value):
    high = value.astype(jnp.bfloat16)
    return high, (value - high.astype(jnp.float32)).astype(jnp.bfloat16)


def split_matmul(a, b, dims):
    dot = functools.partial(
        lax.dot_general, dimension_numbers=(dims, ((), ())), preferred_element_type=jnp.float32
    )
    return dot(a[0], b[0]) + (dot(a[0], b[1]) + dot(a[1], b[0]))


def finish(work, panel_ref, out_ref):
    rows, columns = panel_ref.shape
    part = columns // 2
    for base in (0, part):
        deep = base + part
        factor = halves(work[base : base + part, 0:deep])
        out_ref[:, base : base + part] = split_matmul(
            halves(panel_ref[:, 0:deep]), factor, ((1,), (1,))
        )


def from_gram_kernel(sketch_total, gram_ref, panel_ref, out_ref, work):
    work[...] = add_ridge(gram_ref[...], sketch_total)
    inverse_factor(work)
    finish(work, panel_ref, out_ref)


def flip(index, mask):
    bit = 1
    while bit <= mask:
        if mask & bit:
            index = index + bit - 2 * bit * lax.rem(lax.div(index, bit), 2)
        bit = 2 * bit
    return index


def parity_sign(value, bits):
    span = 1
    while span < bits:
        span = span * 2
    while span > 1:
        span = span // 2
        value = value ^ (value >> span)
    return (1 - 2 * (value & 1)).astype(jnp.float32)


def pivot_rows(block):
    size = block.shape[1]
    lane = lax.broadcasted_iota(jnp.int32, (8, size), 1)
    sub = lax.broadcasted_iota(jnp.int32, (8, size), 0)
    done = []
    for p in range(size // 8):
        base = 8 * p
        tile, below = block[0:8], block[8:]
        cols = [jnp.broadcast_to(tile[:, base + t : base + t + 1], (8, size)) for t in range(8)]
        entry = {
            (u, t): jnp.broadcast_to(cols[t][u : u + 1, :], (8, size)) for t in range(8) for u in range(t, 8)
        }
        tile = jnp.where((lane >= base) & (lane < base + 8), (lane - base == sub).astype(jnp.float32), tile)
        rows = [jnp.broadcast_to(tile[t : t + 1, :], (8, size)) for t in range(8)]
        inverse, ratio = [], {}
        for t in range(8):
            inverse.append(1.0 / entry[t, t])
            for u in range(t + 1, 8):
                ratio[u, t] = entry[u, t] * inverse[t]
            for u in range(t + 1, 8):
                for v in range(t + 1, u + 1):
                    entry[u, v] = entry[u, v] - ratio[u, t] * entry[v, t]
                rows[u] = rows[u] - ratio[u, t] * rows[t]
        own = jnp.zeros((8, size), jnp.float32)
        for t in range(8):
            own = jnp.where(sub == t, rows[t] * lax.rsqrt(entry[t, t]), own)
        done.append(own)
        if base + 8 == size:
            break
        solved = [rows[t] * inverse[t] for t in range(8)]
        for t in range(7, 0, -1):
            for s in range(t):
                solved[s] = solved[s] - ratio[t, s] * solved[t]
        count = below.shape[0]
        wide = lax.broadcasted_iota(jnp.int32, below.shape, 1)
        block = jnp.where((wide >= base) & (wide < base + 8), 0.0, below)
        for t in range(8):
            coef = jnp.broadcast_to(below[:, base + t : base + t + 1], below.shape)
            block = block - coef * jnp.concatenate([solved[t]] * (count // 8), axis=0)
    own = jnp.concatenate(done, axis=0)
    rowi = lax.broadcasted_iota(jnp.int32, (size, size), 0)
    coli = lax.broadcasted_iota(jnp.int32, (size, size), 1)
    return jnp.where(rowi >= coli, own, 0.0)


ODD, EVEN = (7, 3, 5, 1), (6, 2, 4, 0)
LISTS, SLOTS = 14, 26


def sketch_kernel(
    groups, per_owner, scale, sketch_total, panel_hbm, signs_ref, group_ref, row_ref, own_ref, high_ref, low_ref,
    panel_ref, lists, values, split, choice, tables, odd, even, from_core, from_first, from_second, from_group,
    whole, parts_high, parts_low, block, product, loaded, send, recv,
):
    devices = 8
    rows_here, columns = panel_ref.shape
    turns = columns // BLOCK
    band = groups * devices * per_owner
    share = devices * per_owner
    half = band // 2
    left, right = pl.ds(0, half), pl.ds(half, half)
    me = lax.axis_index("dev")
    here = lax.axis_index("grp")
    load = pltpu.make_async_copy(panel_hbm, panel_ref, loaded)
    load.start()

    barrier = pltpu.get_barrier_semaphore()
    for mask in range(1, devices):
        pl.semaphore_signal(
            barrier, inc=1, device_id={"dev": flip(me, mask)}, device_id_type=pl.DeviceIdType.MESH
        )
    for mask in range(1, groups):
        pl.semaphore_signal(
            barrier, inc=1, device_id={"grp": flip(here, mask)}, device_id_type=pl.DeviceIdType.MESH
        )
    pl.semaphore_wait(barrier, devices + groups - 2)

    def remote(source, target, place, axis, mask):
        peer = flip(me if axis == "dev" else here, mask)
        return functools.partial(
            pltpu.make_async_remote_copy,
            src_ref=source,
            dst_ref=target,
            send_sem=send.at[place],
            recv_sem=recv.at[place],
            device_id={axis: peer},
            device_id_type=pl.DeviceIdType.MESH,
        )

    listed = [
        remote(ref, lists.at[kind, mask], kind * 7 + mask - 1, "dev", mask)
        for mask in range(1, devices)
        for kind, ref in enumerate((group_ref, row_ref))
    ]
    for copy in listed:
        copy().start()
    load.wait()
    for turn in range(turns):
        now = panel_ref[:, turn * BLOCK : (turn + 1) * BLOCK]
        top, rest = halves(now)
        split[turn, :, 0:BLOCK] = top
        split[turn, :, BLOCK : 2 * BLOCK] = rest
    lists[0, 0] = group_ref[...]
    lists[1, 0] = row_ref[...]
    for copy in listed:
        copy().wait_recv()

    for slot in range(devices):
        values[slot * groups : (slot + 1) * groups, :] = (
            lists[0, slot] * devices + flip(me, slot)
        ) * rows_here + lists[1, slot]
    total = devices * band
    width = devices * per_owner
    place = lax.broadcasted_iota(jnp.int32, (total, width), 0)
    entry = lax.broadcasted_iota(jnp.int32, (total, width), 1)
    wanted = ((place // band) ^ me) * per_owner + place % per_owner
    spread = lax.dot_general(
        (entry == wanted).astype(jnp.float32),
        values[...].astype(jnp.float32),
        (((1,), (1,)), ((), ())),
        precision=lax.Precision.HIGHEST,
        preferred_element_type=jnp.float32,
    )
    place = lax.broadcasted_iota(jnp.int32, (total, devices * groups), 0)
    held = lax.broadcasted_iota(jnp.int32, (total, devices * groups), 1)
    source = (((place // per_owner) % devices) ^ me) * groups + (((place // share) % groups) ^ here)
    choice[...] = jnp.sum(jnp.where(held == source, spread, 0.0), axis=1, keepdims=True).astype(jnp.int32)

    def table(chunk):
        pick = jnp.broadcast_to(choice[chunk * band : (chunk + 1) * band, :], (band, 128))
        lane = lax.broadcasted_iota(jnp.int32, (band, 128), 1)
        rank = here * devices + me
        above = parity_sign((pick // rows_here) & rank, (groups * devices).bit_length() - 1)
        part = [parity_sign(pick & lane, 7) * above]
        bit = 7
        while 128 * len(part) < rows_here:
            turn = (1 - 2 * ((pick >> bit) & 1)).astype(jnp.float32)
            part = part + [one * turn for one in part]
            bit = bit + 1
        turned = (1 - 2 * signs_ref[...]).astype(jnp.float32)
        part = [(one * turned[i : i + 1, :]).astype(jnp.bfloat16) for i, one in enumerate(part)]
        return jnp.concatenate(part, axis=1)

    def mixed(side, turn):
        both = lax.dot_general(
            tables[side], split[turn], (((1,), (0,)), ((), ())), preferred_element_type=jnp.float32
        )
        return (both[:, 0:BLOCK] + both[:, BLOCK : 2 * BLOCK]).reshape(4, band, BLOCK)

    def at(turn, place):
        return LISTS + SLOTS * turn + place

    def core(t):
        return [remote(odd.at[t, i], from_core.at[t, i], at(t, i), "dev", 1) for i in range(4)]

    def first(t):
        return [
            remote(even.at[t, 0, left], from_first.at[t, 1, left], at(t, 4), "dev", 2),
            remote(even.at[t, 0, right], from_first.at[t, 1, right], at(t, 5), "dev", 4),
            remote(even.at[t, 1, left], from_first.at[t, 0, left], at(t, 6), "dev", 2),
            remote(even.at[t, 2, right], from_first.at[t, 0, right], at(t, 7), "dev", 4),
        ]

    def second(t):
        return [
            remote(even.at[t, 2, left], from_second.at[t, left], at(t, 8), "dev", 4),
            remote(even.at[t, 1, right], from_second.at[t, right], at(t, 9), "dev", 2),
        ]

    def gathered(t):
        return [
            remote(even.at[t, 3, pl.ds(b * share, share)], from_group.at[t, b], at(t, 9 + b), "grp", b)
            for b in range(1, groups)
        ]

    def shared(t):
        mine = whole.at[t, 0, pl.ds(0, share)]
        return [
            remote(mine, whole.at[t, 0, pl.ds(b * share, share)], at(t, 12 + b), "grp", b)
            for b in range(1, groups)
        ]

    def out(t):
        return [
            remote(whole.at[t, 0, left], whole.at[t, 4, left], at(t, 16), "dev", 4),
            remote(whole.at[t, 0, right], whole.at[t, 2, right], at(t, 17), "dev", 2),
            remote(whole.at[t, 0, left], whole.at[t, 2, left], at(t, 18), "dev", 2),
            remote(whole.at[t, 0, right], whole.at[t, 4, right], at(t, 19), "dev", 4),
        ]

    def relay(t):
        return [
            remote(whole.at[t, 4, left], whole.at[t, 6, left], at(t, 20), "dev", 2),
            remote(whole.at[t, 2, right], whole.at[t, 6, right], at(t, 21), "dev", 4),
        ]

    def hand(t):
        return [
            remote(whole.at[t, 2 * i], whole.at[t, 2 * i + 1], at(t, 22 + i), "dev", 1) for i in range(4)
        ]

    def step0(t):
        odd[t] = mixed(0, t)
        for copy in core(t):
            copy().start()

    def step1(t):
        even[t] = mixed(1, t)
        arrived, going = core(t), first(t)
        for i in range(4):
            arrived[i]().wait_recv()
            even[t, i] = even[t, i] + from_core[t, i]
            for copy in (going[0:2], going[2:3], going[3:4], ())[i]:
                copy().start()

    def step2(t):
        arrived, going = first(t), second(t)
        arrived[0]().wait_recv()
        even[t, 2, left] = even[t, 2, left] + from_first[t, 1, left]
        going[0]().start()
        arrived[1]().wait_recv()
        even[t, 1, right] = even[t, 1, right] + from_first[t, 1, right]
        going[1]().start()

    def step3(t):
        for copy in first(t)[2:4] + second(t):
            copy().wait_recv()
        even[t, 3] = even[t, 3] + from_first[t, 0] + from_second[t]
        for copy in gathered(t):
            copy().start()

    def step4(t):
        result = even[t, 3, pl.ds(0, share)]
        for b, copy in enumerate(gathered(t)):
            copy().wait_recv()
            result = result + from_group[t, b + 1]
        whole[t, 0, pl.ds(0, share)] = result * scale
        for copy in shared(t):
            copy().start()
        own_ref[:, t * BLOCK : (t + 1) * BLOCK] = result * scale

    def step5(t):
        for copy in shared(t):
            copy().wait_recv()
        for copy in out(t) + hand(t)[0:1]:
            copy().start()

    def step6(t):
        arrived, on, going = out(t), relay(t), hand(t)
        for i in range(2):
            arrived[i]().wait_recv()
            on[i]().start()
        for i in range(2):
            arrived[2 + i]().wait_recv()
            going[1 + i]().start()

    def step7(t):
        for copy in relay(t):
            copy().wait_recv()
        hand(t)[3]().start()

    def gram_step(k):
        here_k = slice(k * BLOCK, (k + 1) * BLOCK)
        deep = (k + 1) * BLOCK
        now = halves(whole[k].reshape(devices * band, BLOCK))
        parts_high[:, here_k] = now[0]
        parts_low[:, here_k] = now[1]
        gram = split_matmul(now, (parts_high[:, 0:deep], parts_low[:, 0:deep]), ((0,), (0,))) / sketch_total
        rowi = lax.broadcasted_iota(jnp.int32, (BLOCK, BLOCK), 0)
        coli = lax.broadcasted_iota(jnp.int32, (BLOCK, BLOCK), 1)
        corner = gram[:, here_k] + jnp.where(rowi == coli, 0.001, 0.0)
        if k > 0:
            before = k * BLOCK
            known = high_ref[0:before, 0:before], low_ref[0:before, 0:before]
            lower = halves(split_matmul(halves(gram[:, 0:before]), known, ((1,), (1,))))
            corner = corner - split_matmul(lower, lower, ((1,), (1,)))
            product[:, 0:before] = split_matmul(lower, known, ((1,), (0,)))
        block[...] = corner

    def row_step(k):
        here_k = slice(k * BLOCK, (k + 1) * BLOCK)
        own = halves(block[...])
        for target, part in zip((high_ref, low_ref), own):
            target[here_k, here_k] = part
            if k + 1 < turns:
                target[here_k, (k + 1) * BLOCK :] = jnp.zeros((BLOCK, columns - (k + 1) * BLOCK), jnp.bfloat16)
        if k > 0:
            before = k * BLOCK
            rows = halves(-split_matmul(own, halves(product[:, 0:before]), ((1,), (0,))))
            for target, part in zip((high_ref, low_ref), rows):
                target[here_k, 0:before] = part

    for side, chunks in enumerate((ODD, EVEN)):
        for i, chunk in enumerate(chunks):
            tables[side, i * band : (i + 1) * band, :] = table(chunk)
        if side == 0:
            step0(0)
    steps = (step0, step1, step2, step3, step4, step5, step6, step7)
    for tick in range(1, 8):
        for place in range(7, -1, -1):
            if 0 <= tick - place < turns:
                steps[place](tick - place)

    def factor(k, carry):
        for ahead, step in ((1, step7), (2, step6), (3, step5)):
            @pl.when(k + ahead < turns)
            def _(ahead=ahead, step=step):
                step(k + ahead)

        for copy in hand(k):
            copy().wait_recv()
        for place in range(turns):
            @pl.when(k == place)
            def _(place=place):
                gram_step(place)
        block[...] = pivot_rows(block[...])
        for place in range(turns):
            @pl.when(k == place)
            def _(place=place):
                row_step(place)
        return carry

    lax.fori_loop(0, turns, factor, 0)
    for copy in listed:
        copy().wait_send()

    def drain(t, carry):
        for copy in core(t) + first(t) + second(t) + gathered(t) + shared(t) + out(t) + relay(t) + hand(t):
            copy().wait_send()
        return carry

    lax.fori_loop(0, turns, drain, 0)


def kernel_sketch(panel, signs, source_group, source_row, groups, devices):
    rows_here, columns = panel.shape
    per_owner = source_row.shape[2] // devices
    band = groups * devices * per_owner
    share = devices * per_owner
    turns = columns // BLOCK
    scale = 1.0 / math.sqrt(rows_here * devices * groups)
    vmem = pl.BlockSpec(memory_space=pltpu.VMEM)
    f32, bf16 = jnp.float32, jnp.bfloat16
    places = LISTS + SLOTS * turns
    return pl.pallas_call(
        functools.partial(sketch_kernel, groups, per_owner, scale, devices * band),
        out_shape=[
            jax.ShapeDtypeStruct((share, columns), f32),
            jax.ShapeDtypeStruct((columns, columns), bf16),
            jax.ShapeDtypeStruct((columns, columns), bf16),
        ],
        in_specs=[pl.BlockSpec(memory_space=pl.ANY)] + [vmem] * 3,
        out_specs=[vmem] * 3,
        scratch_shapes=[
            pltpu.VMEM((rows_here, columns), f32),
            pltpu.VMEM((2, devices, groups, share), jnp.int32),
            pltpu.VMEM((devices * groups, share), jnp.int32),
            pltpu.VMEM((turns, rows_here, 2 * BLOCK), bf16),
            pltpu.VMEM((devices * band, 1), jnp.int32),
            pltpu.VMEM((2, 4 * band, rows_here), bf16),
            pltpu.VMEM((turns, 4, band, BLOCK), f32),
            pltpu.VMEM((turns, 4, band, BLOCK), f32),
            pltpu.VMEM((turns, 4, band, BLOCK), f32),
            pltpu.VMEM((turns, 2, band, BLOCK), f32),
            pltpu.VMEM((turns, band, BLOCK), f32),
            pltpu.VMEM((turns, groups, share, BLOCK), f32),
            pltpu.VMEM((turns, devices, band, BLOCK), f32),
            pltpu.VMEM((devices * band, columns), bf16),
            pltpu.VMEM((devices * band, columns), bf16),
            pltpu.VMEM((BLOCK, BLOCK), f32),
            pltpu.VMEM((BLOCK, columns), f32),
            pltpu.SemaphoreType.DMA,
            pltpu.SemaphoreType.DMA((places,)),
            pltpu.SemaphoreType.DMA((places,)),
        ],
        compiler_params=pltpu.CompilerParams(collective_id=0, has_side_effects=True),
        name="sketch",
    )(
        panel,
        signs.reshape(rows_here // 128, 128),
        source_group.reshape(groups, share),
        source_row.reshape(groups, share),
    )


def apply_kernel(sketch_ref, high_ref, low_ref, panel_ref, own_ref, out_ref):
    @pl.when(pl.program_id(0) == 0)
    def _():
        own_ref[...] = sketch_ref[...]

    columns = panel_ref.shape[1]
    part = columns // 2
    panel = halves(panel_ref[...])
    for base in (0, part):
        deep = base + part
        factor = high_ref[base:deep, 0:deep], low_ref[base:deep, 0:deep]
        out_ref[:, base:deep] = split_matmul((panel[0][:, 0:deep], panel[1][:, 0:deep]), factor, ((1,), (1,)))


def apply_factor(sketch, high, low, panel):
    rows_here, columns = panel.shape
    part = 256
    fixed = lambda i: (0, 0)
    moving = pl.BlockSpec((part, columns), lambda i: (i, 0))
    once = pl.Buffered(1)
    return pl.pallas_call(
        apply_kernel,
        grid=(rows_here // part,),
        out_shape=[
            jax.ShapeDtypeStruct(sketch.shape, jnp.float32),
            jax.ShapeDtypeStruct(panel.shape, jnp.float32),
        ],
        in_specs=[
            pl.BlockSpec(sketch.shape, fixed, pipeline_mode=once),
            pl.BlockSpec(high.shape, fixed, pipeline_mode=once),
            pl.BlockSpec(low.shape, fixed, pipeline_mode=once),
            moving,
        ],
        out_specs=[pl.BlockSpec(sketch.shape, fixed), moving],
        name="apply",
    )(sketch, high, low, panel)


def bit_parity(value, bits):
    total = jnp.zeros_like(value)
    for bit_place in range(bits):
        total = total + (value >> bit_place & 1)
    return total & 1


def sylvester(order):
    index = jnp.arange(order, dtype=jnp.int32)
    parity = bit_parity(index[:, None] & index[None, :], order.bit_length())
    return (1 - 2 * parity).astype(jnp.float32)


def general_sketch(panel, signs, source_group, source_row):
    rows_here = panel.shape[0]
    columns = panel.shape[1]
    groups = lax.axis_size("grp")
    devices = lax.axis_size("dev")
    group_here = lax.axis_index("grp")
    highest = lax.Precision.HIGHEST
    flipped = panel * (1 - 2 * signs).astype(jnp.float32)[:, None]
    local = jnp.dot(
        sylvester(rows_here), flipped, precision=highest, preferred_element_type=jnp.float32
    )
    dev_table = sylvester(devices)
    mixed = jnp.einsum(
        "ed,dbc->ebc",
        dev_table,
        lax.all_to_all(
            local.reshape(devices, rows_here // devices, columns),
            "dev",
            split_axis=0,
            concat_axis=0,
            tiled=True,
        ),
        precision=highest,
    )
    inner = mixed
    inner = inner.reshape(rows_here, columns)
    chosen_group = source_group[:, 0, :, 0]
    chosen_row = source_row[:, 0, :]
    width = chosen_group.shape[1]
    per_owner = width // devices
    band_size = rows_here // devices
    dev_here = lax.axis_index("dev")
    stacked = jnp.stack([chosen_group, chosen_row]).reshape(2, groups, devices, per_owner)
    lists = lax.all_to_all(stacked, "dev", split_axis=2, concat_axis=2, tiled=True)
    band_group = lists[0].reshape(-1)
    band_row = lists[1].reshape(-1)
    flat_place = jnp.arange(groups * devices * per_owner, dtype=jnp.int32)
    source_dev = flat_place // per_owner % devices
    flat_index = source_dev * band_size + band_row - dev_here * band_size
    parity = bit_parity(band_group & group_here, groups.bit_length())
    factor = (1 - 2 * parity).astype(jnp.float32)
    gathered = lax.psum_scatter(
        inner[flat_index] * factor[:, None], "grp", scatter_dimension=0, tiled=True
    )
    panel_total = rows_here * devices * groups
    sketch = gathered * (1.0 / math.sqrt(panel_total))
    sketch_total = sketch.shape[0] * devices * groups
    partial_gram = jnp.dot(sketch.T, sketch, precision=highest, preferred_element_type=jnp.float32)
    return sketch, lax.psum(partial_gram, ("grp", "dev"))


def on_device(panel, signs, source_group, source_row):
    rows_here, columns = panel.shape
    groups = lax.axis_size("grp")
    devices = lax.axis_size("dev")
    width = source_row.shape[2]
    sketch_total = groups * devices * width
    fits = groups == 4 and devices == 8 and groups * width == BLOCK
    if fits and columns == 4 * BLOCK and rows_here % 256 == 0 and rows_here & (rows_here - 1) == 0:
        sketch, high, low = kernel_sketch(panel, signs, source_group, source_row, groups, devices)
        sketch, conditioned = apply_factor(sketch, high, low, panel)
        return (sketch, conditioned)
    sketch, gram = general_sketch(panel, signs, source_group, source_row)
    conditioned = pl.pallas_call(
        functools.partial(from_gram_kernel, sketch_total),
        out_shape=jax.ShapeDtypeStruct((rows_here, columns), jnp.float32),
        in_specs=[pl.BlockSpec(memory_space=pltpu.VMEM)] * 2,
        out_specs=pl.BlockSpec(memory_space=pltpu.VMEM),
        scratch_shapes=[pltpu.VMEM((columns, columns), jnp.float32)],
        name="factor",
    )(gram, panel)
    return (sketch, conditioned)


def solution(mesh):
    return jax.shard_map(
        on_device,
        mesh=mesh,
        in_specs=(
            P(("grp", "dev"), None),
            P(("grp", "dev")),
            P(None, "dev", None, None),
            P(None, "dev", None),
        ),
        out_specs=(P(("grp", "dev"), None), P(("grp", "dev"), None)),
        check_vma=False,
    )
```

time: 76.3 us -> 73.6 us (0.965)
  Pallas kernels: 75.5 us -> 72.7 us
    pallas_call x2, Pallas kernels: 75.5 us -> 72.7 us  [the longest x1 67.6 us: kernel_sketch(): pl.pallas_call(functools.partial(sketch_kernel, groups, per_owner, scale,...]
where the time goes in v1:
time: 73.6 us; the launch traced here: 73.4 us
  Pallas kernels  72.7 us (99%)
    pallas_call x1, Pallas kernels, kernel_sketch(): pl.pallas_call(functools.partial(sketch_kernel, groups, per_owner, scale,...  67.6 us
    pallas_call x1, Pallas kernels, apply_factor(): pl.pallas_call(apply_kernel, grid=(rows_here // part,), out_shape=[jax.Sh...  5.1 us

profile of v1, /device:TPU:0, one launch (start us, length us, event | category | flops | bytes accessed | tf_op | source)
XLA Modules:
  0.0 73.4 jit_solution(6597291966368826096)
XLA Ops:
  0.6 67.6 %sketch.1 = (f32[32,512]{1,0:T(8,128)}, bf16[512,512]{1,0:T(8,128)(2,1)}, bf16[512,512]{1,0:T(8,128)(2,1)}) custom-call(f32[1024,512]{1,0:T(8,128)} %panel_ref.1, s32[8,128]{1,0:T(8,128)} %bitcast.3, s32[4,32]{1,0:T(4,128)} %bitcast.4, s32[4,32]{1,0:T(4,128)} %bitcast.5), custom_call_target="tpu_custom_call" | custom-call | tf_op jit(solution)/shard_map/sketch/pallas_call | solution.py:480
  68.3 5.1 %apply.1 = (f32[32,512]{1,0:T(8,128)}, f32[1024,512]{1,0:T(8,128)}) custom-call(f32[32,512]{1,0:T(8,128)} %get-tuple-element.5.sketch_ref, bf16[512,512]{1,0:T(8,128)(2,1)} %get-tuple-element.6.high_ref, bf16[512,512]{1,0:T(8,128)(2,1)} %get-tuple-element.7.low_ref, f32[1024,512]{1,0:T(8,128)} %panel_ref.1), custom_call_target="tpu_custom_call" | custom-call | tf_op jit(solution)/shard_map/apply/pallas_call | solution.py:541

commit v2 on v1

--- a/solution.py
+++ b/solution.py
@@ -133,13 +133,19 @@
     return (1 - 2 * (value & 1)).astype(jnp.float32)
 
 
-def pivot_rows(block):
+ODD, EVEN = (7, 3, 5, 1), (6, 2, 4, 0)
+LISTS, SLOTS, MIDDLE = 14, 20, 9
+
+
+def pivot_rows(block, halfway):
     size = block.shape[1]
     lane = lax.broadcasted_iota(jnp.int32, (8, size), 1)
     sub = lax.broadcasted_iota(jnp.int32, (8, size), 0)
     done = []
     for p in range(size // 8):
         base = 8 * p
+        if p == MIDDLE:
+            halfway()
         tile, below = block[0:8], block[8:]
         cols = [jnp.broadcast_to(tile[:, base + t : base + t + 1], (8, size)) for t in range(8)]
         entry = {
@@ -178,13 +184,9 @@
     return jnp.where(rowi >= coli, own, 0.0)
 
 
-ODD, EVEN = (7, 3, 5, 1), (6, 2, 4, 0)
-LISTS, SLOTS = 14, 26
-
-
 def sketch_kernel(
     groups, per_owner, scale, sketch_total, panel_hbm, signs_ref, group_ref, row_ref, own_ref, high_ref, low_ref,
-    panel_ref, lists, values, split, choice, tables, odd, even, from_core, from_first, from_second, from_group,
+    panel_ref, lists, values, split, choice, tables, odd, even, from_core, from_first, from_group,
     whole, parts_high, parts_low, block, product, loaded, send, recv,
 ):
     devices = 8
@@ -192,8 +194,6 @@
     turns = columns // BLOCK
     band = groups * devices * per_owner
     share = devices * per_owner
-    half = band // 2
-    left, right = pl.ds(0, half), pl.ds(half, half)
     me = lax.axis_index("dev")
     here = lax.axis_index("grp")
     load = pltpu.make_async_copy(panel_hbm, panel_ref, loaded)
@@ -290,109 +290,75 @@
 
     def first(t):
         return [
-            remote(even.at[t, 0, left], from_first.at[t, 1, left], at(t, 4), "dev", 2),
-            remote(even.at[t, 0, right], from_first.at[t, 1, right], at(t, 5), "dev", 4),
-            remote(even.at[t, 1, left], from_first.at[t, 0, left], at(t, 6), "dev", 2),
-            remote(even.at[t, 2, right], from_first.at[t, 0, right], at(t, 7), "dev", 4),
-        ]
-
-    def second(t):
-        return [
-            remote(even.at[t, 2, left], from_second.at[t, left], at(t, 8), "dev", 4),
-            remote(even.at[t, 1, right], from_second.at[t, right], at(t, 9), "dev", 2),
+            remote(even.at[t, i], from_first.at[t, i], at(t, 4 + i), "dev", mask)
+            for i, mask in enumerate(EVEN[0:3])
         ]
 
     def gathered(t):
         return [
-            remote(even.at[t, 3, pl.ds(b * share, share)], from_group.at[t, b], at(t, 9 + b), "grp", b)
-            for b in range(1, groups)
+            remote(even.at[t, 3, pl.ds(b * share, share)], from_group.at[t, b], at(t, 6 + b), "grp", b)
+            for b in (3, 2, 1)
         ]
 
     def shared(t):
         mine = whole.at[t, 0, pl.ds(0, share)]
         return [
-            remote(mine, whole.at[t, 0, pl.ds(b * share, share)], at(t, 12 + b), "grp", b)
-            for b in range(1, groups)
+            remote(mine, whole.at[t, 0, pl.ds(b * share, share)], at(t, 9 + b), "grp", b)
+            for b in (3, 2, 1)
         ]
 
     def out(t):
         return [
-            remote(whole.at[t, 0, left], whole.at[t, 4, left], at(t, 16), "dev", 4),
-            remote(whole.at[t, 0, right], whole.at[t, 2, right], at(t, 17), "dev", 2),
-            remote(whole.at[t, 0, left], whole.at[t, 2, left], at(t, 18), "dev", 2),
-            remote(whole.at[t, 0, right], whole.at[t, 4, right], at(t, 19), "dev", 4),
-        ]
-
-    def relay(t):
-        return [
-            remote(whole.at[t, 4, left], whole.at[t, 6, left], at(t, 20), "dev", 2),
-            remote(whole.at[t, 2, right], whole.at[t, 6, right], at(t, 21), "dev", 4),
+            remote(whole.at[t, 0], whole.at[t, mask], at(t, 13 + i), "dev", mask)
+            for i, mask in enumerate(EVEN[0:3])
         ]
 
     def hand(t):
         return [
-            remote(whole.at[t, 2 * i], whole.at[t, 2 * i + 1], at(t, 22 + i), "dev", 1) for i in range(4)
+            remote(whole.at[t, mask], whole.at[t, mask + 1], at(t, 16 + i), "dev", 1)
+            for i, mask in enumerate(EVEN)
         ]
 
-    def step0(t):
+    def start_core(t):
         odd[t] = mixed(0, t)
         for copy in core(t):
             copy().start()
 
-    def step1(t):
+    def start_first(t):
+        arrived, going = core(t), first(t)
         even[t] = mixed(1, t)
-        arrived, going = core(t), first(t)
         for i in range(4):
             arrived[i]().wait_recv()
             even[t, i] = even[t, i] + from_core[t, i]
-            for copy in (going[0:2], going[2:3], going[3:4], ())[i]:
-                copy().start()
-
-    def step2(t):
-        arrived, going = first(t), second(t)
-        arrived[0]().wait_recv()
-        even[t, 2, left] = even[t, 2, left] + from_first[t, 1, left]
-        going[0]().start()
-        arrived[1]().wait_recv()
-        even[t, 1, right] = even[t, 1, right] + from_first[t, 1, right]
-        going[1]().start()
-
-    def step3(t):
-        for copy in first(t)[2:4] + second(t):
+            if i < 3:
+                going[i]().start()
+
+    def start_gather(t):
+        for copy in first(t):
             copy().wait_recv()
-        even[t, 3] = even[t, 3] + from_first[t, 0] + from_second[t]
+        even[t, 3] = even[t, 3] + from_first[t, 0] + (from_first[t, 1] + from_first[t, 2])
         for copy in gathered(t):
             copy().start()
 
-    def step4(t):
-        result = even[t, 3, pl.ds(0, share)]
-        for b, copy in enumerate(gathered(t)):
+    def start_share(t):
+        for copy in gathered(t):
             copy().wait_recv()
-            result = result + from_group[t, b + 1]
+        result = even[t, 3, pl.ds(0, share)] + from_group[t, 1] + (from_group[t, 2] + from_group[t, 3])
         whole[t, 0, pl.ds(0, share)] = result * scale
         for copy in shared(t):
             copy().start()
         own_ref[:, t * BLOCK : (t + 1) * BLOCK] = result * scale
 
-    def step5(t):
+    def start_out(t):
         for copy in shared(t):
             copy().wait_recv()
-        for copy in out(t) + hand(t)[0:1]:
+        for copy in out(t) + hand(t)[3:4]:
             copy().start()
 
-    def step6(t):
-        arrived, on, going = out(t), relay(t), hand(t)
-        for i in range(2):
-            arrived[i]().wait_recv()
-            on[i]().start()
-        for i in range(2):
-            arrived[2 + i]().wait_recv()
-            going[1 + i]().start()
-
-    def step7(t):
-        for copy in relay(t):
+    def start_hand(t):
+        for copy, on in zip(out(t), hand(t)):
             copy().wait_recv()
-        hand(t)[3]().start()
+            on().start()
 
     def gram_step(k):
         here_k = slice(k * BLOCK, (k + 1) * BLOCK)
@@ -429,18 +395,27 @@
         for i, chunk in enumerate(chunks):
             tables[side, i * band : (i + 1) * band, :] = table(chunk)
         if side == 0:
-            step0(0)
-    steps = (step0, step1, step2, step3, step4, step5, step6, step7)
-    for tick in range(1, 8):
-        for place in range(7, -1, -1):
-            if 0 <= tick - place < turns:
-                steps[place](tick - place)
+            start_core(0)
+    start_first(0)
+    for turn in range(1, turns):
+        start_core(turn)
+        start_first(turn)
+    for step, turn in (
+        (start_gather, 0), (start_gather, 1), (start_share, 0), (start_gather, 2), (start_share, 1),
+        (start_gather, 3), (start_out, 0), (start_share, 2), (start_out, 1), (start_share, 3),
+        (start_hand, 0), (start_out, 2),
+    ):
+        step(turn)
 
     def factor(k, carry):
-        for ahead, step in ((1, step7), (2, step6), (3, step5)):
-            @pl.when(k + ahead < turns)
-            def _(ahead=ahead, step=step):
-                step(k + ahead)
+        def halfway():
+            @pl.when(k == 0)
+            def _():
+                start_out(3)
+
+            @pl.when(k + 1 < turns)
+            def _():
+                start_hand(k + 1)
 
         for copy in hand(k):
             copy().wait_recv()
@@ -448,7 +423,7 @@
             @pl.when(k == place)
             def _(place=place):
                 gram_step(place)
-        block[...] = pivot_rows(block[...])
+        block[...] = pivot_rows(block[...], halfway)
         for place in range(turns):
             @pl.when(k == place)
             def _(place=place):
@@ -460,7 +435,7 @@
         copy().wait_send()
 
     def drain(t, carry):
-        for copy in core(t) + first(t) + second(t) + gathered(t) + shared(t) + out(t) + relay(t) + hand(t):
+        for copy in core(t) + first(t) + gathered(t) + shared(t) + out(t) + hand(t):
             copy().wait_send()
         return carry
 
@@ -496,8 +471,7 @@
             pltpu.VMEM((turns, 4, band, BLOCK), f32),
             pltpu.VMEM((turns, 4, band, BLOCK), f32),
             pltpu.VMEM((turns, 4, band, BLOCK), f32),
-            pltpu.VMEM((turns, 2, band, BLOCK), f32),
-            pltpu.VMEM((turns, band, BLOCK), f32),
+            pltpu.VMEM((turns, 3, band, BLOCK), f32),
             pltpu.VMEM((turns, groups, share, BLOCK), f32),
             pltpu.VMEM((turns, devices, band, BLOCK), f32),
             pltpu.VMEM((devices * band, columns), bf16),

time: 73.6 us -> 61.5 us (0.84)
  Pallas kernels: 72.7 us -> 60.4 us
    pallas_call x1, Pallas kernels: 67.6 us -> 55.4 us  [kernel_sketch(): pl.pallas_call(functools.partial(sketch_kernel, groups, per_owner, scale,...]
where the time goes in v2:
time: 61.5 us; the launch traced here: 61.1 us
  Pallas kernels  60.4 us (98%)
  between operations  0.64 us (1%)
    pallas_call x1, Pallas kernels, kernel_sketch(): pl.pallas_call(functools.partial(sketch_kernel, groups, per_owner, scale,...  55.4 us
    pallas_call x1, Pallas kernels, apply_factor(): pl.pallas_call(apply_kernel, grid=(rows_here // part,), out_shape=[jax.Sh...  5.1 us

profile of v2, /device:TPU:0, one launch (start us, length us, event | category | flops | bytes accessed | tf_op | source)
XLA Modules:
  0.0 61.1 jit_solution(243309640394160508)
XLA Ops:
  0.6 55.4 %sketch.1 = (f32[32,512]{1,0:T(8,128)}, bf16[512,512]{1,0:T(8,128)(2,1)}, bf16[512,512]{1,0:T(8,128)(2,1)}) custom-call(f32[1024,512]{1,0:T(8,128)} %panel_ref.1, s32[8,128]{1,0:T(8,128)} %bitcast.3, s32[4,32]{1,0:T(4,128)} %bitcast.4, s32[4,32]{1,0:T(4,128)} %bitcast.5), custom_call_target="tpu_custom_call" | custom-call | tf_op jit(solution)/shard_map/sketch/pallas_call | solution.py:455
  56.0 5.1 %apply.1 = (f32[32,512]{1,0:T(8,128)}, f32[1024,512]{1,0:T(8,128)}) custom-call(f32[32,512]{1,0:T(8,128)} %get-tuple-element.5.sketch_ref, bf16[512,512]{1,0:T(8,128)(2,1)} %get-tuple-element.6.high_ref, bf16[512,512]{1,0:T(8,128)(2,1)} %get-tuple-element.7.low_ref, f32[1024,512]{1,0:T(8,128)} %panel_ref.1), custom_call_target="tpu_custom_call" | custom-call | tf_op jit(solution)/shard_map/apply/pallas_call | solution.py:515
